TPU v7x, 32 devices: a whole 2x2x4 slice. The times are simulated.
32 devices in a mesh: groups: 2 (over y), seq: 4 (over z), inner: 2 (over x), head: 2 (over core).
Axes of the slice: x: 2, y: 2, z: 4, core: 2. Of those that a mesh axis runs over, the one named last changes fastest.
Arguments:
- queries: bfloat16 [2048, 32, 128], P(('groups', 'seq', 'inner'), 'head'), parts along dimension 0, as said below
- keys: bfloat16 [2048, 4, 128], P(('groups', 'seq', 'inner'), 'head'), parts along dimension 0
- values: bfloat16 [2048, 4, 128], P(('groups', 'seq', 'inner'), 'head'), parts along dimension 0, may hold values from -6 to 6
- log_decay: float32 [2048, 4], P(('groups', 'seq', 'inner'), 'head'), parts along dimension 0, as said below
- gain: float32 [32, 128], P('head'), may hold values from 0.1 to 1.9
- block_list: int32 [32, 16], P(('groups', 'seq', 'inner')), parts along dimension 0, may hold values from 0 to 15, as said below
Outputs:
- attended: bfloat16 [2048, 32, 128], P(('groups', 'seq', 'inner'), 'head'), parts along dimension 0
There are 2 independent parts, one for each index of `groups`. A program takes and returns all parts, laid end to end along the dimension named above; an argument that names none is the same for every part. Nothing has to cross between parts.
Inputs may be any that keep to these rules, and one draw needn't show every extreme that they name: Keys lie within -6 to 6; queries within -144 to 144. `log_decay`: each entry is below 0. `block_list`: entry 0 of row b is b. The sequence's pieces of 128 tokens fall into segments: piece p belongs to segment p modulo 2. Every entry of row b is a block at or before b in a piece of b's segment.
All inputs are finite; a program needn't handle non-finite values.
Results may differ from a plain program's by a relative error of at most 0.0017.
Values may be sent and summed in bfloat16 or wider, within the bound.
A program may use at most 64 MiB of HBM per device.

v0:
```python
import jax
import jax.numpy as jnp
from jax import lax
from jax.sharding import PartitionSpec as P

BLK = 64
SEL = 16
HIGH = lax.Precision.HIGHEST


def prefix(shard, axis, combine, identity):
    devices, here = (lax.axis_size(axis), lax.axis_index(axis))
    everything = jax.tree.map(lambda part: lax.all_gather(part, axis), shard)
    start = jax.tree.map(
        lambda part, zero: jnp.broadcast_to(jnp.asarray(zero, part.dtype), part.shape),
        shard,
        identity,
    )

    def turn(k, before):
        reached = k < here
        new = combine(before, jax.tree.map(lambda part: part[k], everything))
        return jax.tree.map(lambda a, b: jnp.where(reached, a, b), new, before)

    return lax.fori_loop(0, devices, turn, start)


def combine(earlier, later):
    return (earlier[0] * later[0], later[0][:, None, None] * earlier[1] + later[1])


def shards(queries, keys, values, log_decay, gain, block_list):
    tokens, heads_loc, width = queries.shape
    kv_loc = keys.shape[1]
    rep = heads_loc // kv_loc
    qf = queries.astype(jnp.float32).reshape(tokens, kv_loc, rep, width)
    kf = keys.astype(jnp.float32)
    vf = values.astype(jnp.float32)
    cum = jnp.cumsum(log_decay, axis=0)
    total = cum[-1]
    causal = jnp.arange(tokens)[:, None] >= jnp.arange(tokens)[None, :]
    scores = jnp.einsum("tkrd,skd->krts", qf, kf, precision=HIGH)
    diff = cum.T[:, :, None] - cum.T[:, None, :]
    weight = jnp.where(causal[None], jnp.exp(jnp.minimum(diff, 0.0)), 0.0)
    intra = jnp.einsum("krts,skd->tkrd", scores * weight[:, None], vf, precision=HIGH)
    tail = jnp.exp(total[None, :] - cum)
    own_state = jnp.einsum("skd,ske->kde", kf * tail[:, :, None], vf, precision=HIGH)
    own_decay = jnp.exp(total)
    identity = (jnp.ones_like(own_decay), jnp.zeros_like(own_state))
    prior = prefix((own_decay, own_state), ("seq", "inner"), combine, identity)
    prior_state = prior[1]
    inter = jnp.exp(cum)[:, :, None, None] * jnp.einsum(
        "tkrd,kde->tkre", qf, prior_state, precision=HIGH
    )
    linear = (intra + inter).reshape(tokens, heads_loc, width)
    normed = (
        linear * lax.rsqrt(jnp.mean(linear * linear, axis=-1, keepdims=True) + 1e-06) * gain[None]
    )
    per_piece = tokens // BLK
    n_inner = lax.axis_size("inner")
    start_pos = (lax.axis_index("seq") * n_inner + lax.axis_index("inner")) * tokens
    seg_block = block_list // (n_inner * per_piece) * per_piece + block_list % per_piece
    seg_keys, seg_values = (
        lax.all_gather(keys, "seq", axis=0, tiled=True),
        lax.all_gather(values, "seq", axis=0, tiled=True),
    )
    key_blocks = seg_keys.reshape(-1, BLK, kv_loc, width)
    value_blocks = seg_values.reshape(-1, BLK, kv_loc, width)
    picked_keys = key_blocks[seg_block]
    picked_values = value_blocks[seg_block]
    lower = jnp.arange(SEL)[None, :] < jnp.arange(SEL)[:, None]
    repeat = jnp.any((block_list[:, :, None] == block_list[:, None, :]) & lower[None], axis=2)
    keep_all = jnp.logical_not(repeat)
    query_pos = start_pos + jnp.arange(tokens).reshape(per_piece, BLK)
    key_pos = block_list[:, :, None] * BLK + jnp.arange(BLK)[None, None, :]
    q_blocks = queries.reshape(per_piece, BLK, kv_loc, rep, width)

    def one_block(args):
        qblk, pk, pv, qpos, kpos, keep = args
        valid = keep[None, :, None] & (kpos[None] <= qpos[:, None, None])
        score = jnp.einsum(
            "qkrd,jukd->krqju", qblk, pk, preferred_element_type=jnp.float32
        ) * width ** (-0.5)
        score = jnp.where(valid[None, None], score, -1e30)
        top = jnp.max(score, axis=(3, 4), keepdims=True)
        expo = jnp.where(valid[None, None], jnp.exp(score - top), 0.0)
        denom = jnp.sum(expo, axis=(3, 4))
        weights = expo.astype(jnp.bfloat16)
        out = jnp.einsum("krqju,jukd->qkrd", weights, pv, preferred_element_type=jnp.float32)
        return out / jnp.transpose(denom, (2, 0, 1))[:, :, :, None]

    outs = lax.map(one_block, (q_blocks, picked_keys, picked_values, query_pos, key_pos, keep_all))
    sparse = outs.reshape(tokens, heads_loc, width)
    return (normed + sparse).astype(jnp.bfloat16)


def solution(mesh):
    return jax.shard_map(
        shards,
        mesh=mesh,
        in_specs=(
            P(("groups", "seq", "inner"), "head", None),
            P(("groups", "seq", "inner"), "head", None),
            P(("groups", "seq", "inner"), "head", None),
            P(("groups", "seq", "inner"), "head"),
            P("head", None),
            P(("groups", "seq", "inner"), None),
        ),
        out_specs=P(("groups", "seq", "inner"), "head", None),
        check_vma=False,
    )
```

profile of v0, /device:TPU:0, one launch (start us, length us, event | category | flops | bytes accessed | tf_op | source)
XLA Modules:
  0.0 109.6 jit_solution(16745564901405145584)
XLA Ops:
  8.1 1.0 convert_multiply_fusion
  9.2 1.8 %fusion.30 = f32[2,128,128]{2,1,0:T(8,128)} fusion(f32[128,2,128]{2,1,0:T(2,128)S(1)} %convert_multiply_fusion, bf16[128,2,128]{2,1,0:T(2,128)(2,1)} %param.12), kind=kOutput, calls=%fused_computation.44 | convolution fusion | flops 50331648 | bytes 327680 | tf_op jit(solution)/shard_map/skd,ske->kde/dot_general | solution.py:47
  12.7 16.1 %all_gather.19 = bf16[512,2,128]{2,0,1:T(8,128)(2,1)S(1)} all-gather(bf16[128,2,128]{2,0,1:T(8,128)(2,1)S(1)} %copy.121), channel_id=1, replica_groups=mesh['groups'=2,'seq'=4,'inner'=2,'head'=2] {'seq'}, dimensions={0}, use_global_device_ids=true | all-gather | bytes 327680 | tf_op jit(solution)/shard_map/all_gather | solution.py:65
  31.8 15.7 %all_gather.20 = bf16[512,2,128]{2,0,1:T(8,128)(2,1)S(1)} all-gather(bf16[128,2,128]{2,0,1:T(8,128)(2,1)S(1)} %copy.129), channel_id=1, replica_groups=mesh['groups'=2,'seq'=4,'inner'=2,'head'=2] {'seq'}, dimensions={0}, use_global_device_ids=true | all-gather | bytes 327680 | tf_op jit(solution)/shard_map/all_gather | solution.py:64
  49.2 18.8 %while.24 = (s32[]{:T(128)}, f32[2,64,2,8,128]{4,3,2,1,0:T(8,128)S(1)}, bf16[2,16,64,2,128]{4,2,3,1,0:T(8,128)(2,1)S(1)}, pred[2,16]{1,0:T(4,128)(4,1)}, s32[2,1...) while((s32[]{:T(128)}, ...), condition=%wide.region_8.9_spmd, body=%wide.region_5.8_spmd.sunk | while | flops 550762496 | bytes 18383788 | solution.py:92
  51.8 1.8 %fusion.49 = (f32[2,8,64]{2,1,0:T(8,128)S(1)}, f32[2,16,64,64,8]{3,2,4,1,0:T(8,128)S(1)}) fusion(pred[64,16,64]{0,2,1:T(8,128)(4,1)S(1)} %compare_and_fusion.2, bf16[1,64,2,8,128]{4,3,2,1,0:T(8,128)(2,1)S(1)} %constant_dynamic-slice_fusion.7, bf16[1,16,64,2,128]{4,2,3,1,0:T(8,128)(2,1)S(1)} %get-tuple-element.348), kind=kOutput, calls=%fused_computation.4.clone.1 | convolution fusion | flops 271580160 | bytes 5050368 | tf_op jit(solution)/shard_map/while/body/eval_jaxpr/qkrd,jukd->krqju/dot_general | solution.py:81
  53.6 2.3 %fusion.50 = f32[2,8,64]{2,1,0:T(8,128)S(1)} fusion(f32[2,16,64,64,8]{3,2,4,1,0:T(8,128)S(1)} %get-tuple-element.349, f32[2,8,64]{2,1,0:T(8,128)S(1)} %get-tuple-element.350, pred[64,16,64]{0,2,1:T(8,128)(4,1)S(1)} %compare_and_fusion.2), kind=kLoop, calls=%fused_computation.5.clone.1 | loop fusion | flops 5241856 | bytes 4268032 | tf_op jit(solution)/shard_map/while/body/eval_jaxpr/reduce_sum | solution.py:87
  55.9 2.3 %fusion.51 = f32[1,64,2,8,128]{4,1,3,2,0:T(8,128)S(1)} fusion(f32[2,16,64,64,8]{3,2,4,1,0:T(8,128)S(1)} %get-tuple-element.349, f32[2,8,64]{2,1,0:T(8,128)S(1)} %get-tuple-element.350, pred[64,16,64]{0,2,1:T(8,128)(4,1)S(1)} %compare_and_fusion.2, bf16[1,16,64,2,128]{4,2,3,1,0:T(8,128)(2,1)S(1)} %get-tuple-element.351, f32[64,2,8]{0,2,1:T(8,128)S(1)} %bitcast.148), kind=kOutput, calls=%fused_computation.11.clone.1 | convolution fusion | flops 273809408 | bytes 5316608 | tf_op jit(solution)/shard_map/while/body/eval_jaxpr/krqju,jukd->qkrd/dot_general | solution.py:89
  61.2 1.8 %fusion.49 = (f32[2,8,64]{2,1,0:T(8,128)S(1)}, f32[2,16,64,64,8]{3,2,4,1,0:T(8,128)S(1)}) fusion(pred[64,16,64]{0,2,1:T(8,128)(4,1)S(1)} %compare_and_fusion.2, bf16[1,64,2,8,128]{4,3,2,1,0:T(8,128)(2,1)S(1)} %constant_dynamic-slice_fusion.7, bf16[1,16,64,2,128]{4,2,3,1,0:T(8,128)(2,1)S(1)} %get-tuple-element.348), kind=kOutput, calls=%fused_computation.4.clone.1 | convolution fusion | flops 271580160 | bytes 5050368 | tf_op jit(solution)/shard_map/while/body/eval_jaxpr/qkrd,jukd->krqju/dot_general | solution.py:81
  63.0 2.3 %fusion.50 = f32[2,8,64]{2,1,0:T(8,128)S(1)} fusion(f32[2,16,64,64,8]{3,2,4,1,0:T(8,128)S(1)} %get-tuple-element.349, f32[2,8,64]{2,1,0:T(8,128)S(1)} %get-tuple-element.350, pred[64,16,64]{0,2,1:T(8,128)(4,1)S(1)} %compare_and_fusion.2), kind=kLoop, calls=%fused_computation.5.clone.1 | loop fusion | flops 5241856 | bytes 4268032 | tf_op jit(solution)/shard_map/while/body/eval_jaxpr/reduce_sum | solution.py:87
  65.3 2.3 %fusion.51 = f32[1,64,2,8,128]{4,1,3,2,0:T(8,128)S(1)} fusion(f32[2,16,64,64,8]{3,2,4,1,0:T(8,128)S(1)} %get-tuple-element.349, f32[2,8,64]{2,1,0:T(8,128)S(1)} %get-tuple-element.350, pred[64,16,64]{0,2,1:T(8,128)(4,1)S(1)} %compare_and_fusion.2, bf16[1,16,64,2,128]{4,2,3,1,0:T(8,128)(2,1)S(1)} %get-tuple-element.351, f32[64,2,8]{0,2,1:T(8,128)S(1)} %bitcast.148), kind=kOutput, calls=%fused_computation.11.clone.1 | convolution fusion | flops 273809408 | bytes 5316608 | tf_op jit(solution)/shard_map/while/body/eval_jaxpr/krqju,jukd->qkrd/dot_general | solution.py:89
  68.0 20.6 %all-gather.1 = f32[8,1,2]{2,1,0:T(1,128)S(1)} all-gather(f32[1,1,2]{2,1,0:T(1,128)S(1)} %copy-done.4), channel_id=1, replica_groups=mesh['groups'=2,'seq'=4,'inner'=2,'head'=2] {'seq','inner'}, dimensions={0}, use_global_device_ids=true | all-gather | bytes 72 | tf_op jit(solution)/shard_map/all_gather | solution.py:13
  88.9 1.4 %fusion.26 = f32[2,8,128,128]{2,3,1,0:T(8,128)S(1)} fusion(f32[2,128,128]{1,2,0:T(8,128)S(1)} %exponential_select_fusion.1, bf16[128,2,8,128]{3,2,1,0:T(8,128)(2,1)} %bitcast.138, bf16[128,2,128,1]{2,1,0,3:T(2,128)(2,1)S(1)} %bitcast.144), kind=kOutput, calls=%fused_computation.38 | convolution fusion | flops 67371008 | bytes 1769472 | tf_op jit(solution)/shard_map/tkrd,skd->krts/dot_general | solution.py:42
  91.0 8.3 %while.25 = (s32[]{:T(128)}, f32[2,128,128]{2,1,0:T(8,128)S(1)}, s32[]{:T(128)}, f32[8,2]{1,0:T(8,128)S(1)}, f32[8,2,128,128]{3,2,1,0:T(8,128)}, /*index=5*/s32[]{:T(128)}, s32[]{:T(128)}) while((s32[]{:T(128)}, f32[2,128,128]{2,1,0:T(8,128)S(1)}, s32[]{:T(128)}, f32[8,2]{1,0:T(8,128)S(1)}, f32[8,2,128,128]{3,2,1,0:T(8,128)}, ...), condition=%wide.region_2.3_spmd.clone, body=%wide.region_1.2_spmd.clone.sunk | while | flops 131076 | bytes 393353 | solution.py:25
  91.0 1.0 fusion.52
  92.0 1.0 fusion.52
  93.1 1.0 fusion.52
  94.1 1.0 fusion.52
  95.1 1.0 fusion.52
  96.2 1.0 fusion.52
  97.2 1.0 fusion.52
  98.2 1.0 fusion.52
  99.2 1.8 %multiply_reduce_fusion = (f32[128,2,8]{0,2,1:T(8,128)S(1)}, f32[128,2,8,128]{0,3,2,1:T(8,128)S(1)}) fusion(f32[128,2,8,128]{0,3,2,1:T(8,128)S(1)} %convolution_bitcast_fusion.2, bf16[128,2,8,128]{3,2,1,0:T(8,128)(2,1)} %bitcast.139, f32[2,128,128]{2,1,0:T(8,128)S(1)} %get-tuple-element.141, f32[128,2]{0,1:T(2,128)S(1)} %copy.118), kind=kOutput, calls=%fused_computation.40 | convolution fusion | flops 403699712 | bytes 2761728 | tf_op jit(solution)/shard_map/tkrd,kde->tkre/dot_general | solution.py:52
  101.6 1.1 %add_convert_fusion = bf16[128,16,128]{2,1,0:T(8,128)(2,1)} fusion(f32[128,16,128]{2,1,0:T(8,128)S(1)} %bitcast.143, f32[128,16,128]{2,1,0:T(8,128)S(1)} %copy.126, f32[16,128]{1,0:T(8,128)S(1)} %copy-done.3, f32[128,16]{1,0:T(8,128)S(1)} %copy.125), kind=kLoop, calls=%fused_computation.39 | loop fusion | flops 1048576 | bytes 2637824 | tf_op jit(solution)/shard_map/convert_element_type | solution.py:94
  (63 shorter events, 15.6 us)
Async XLA Ops:
  6.5 84.4 %all-gather.4.cloned.1.call-start = ((), (), s32[]{:S(2)}) async-start(), calls=%async_computation | async-start | bytes 1179648 | tf_op jit(solution)/shard_map/all_gather | solution.py:13
  29.6 17.9 %copy-start.2 = (s32[1024]{0:T(1024)}, s32[1024]{0:T(1024)S(1)}, u32[]{:S(2)}) copy-start(s32[1024]{0:T(1024)S(1)} %pad_clamp_fusion) | copy-start | bytes 12292
  49.1 18.8 %copy-start.4 = (f32[1,1,2]{2,1,0:T(1,128)S(1)}, f32[1,1,2]{2,1,0:T(1,128)}, u32[]{:S(2)}) copy-start(f32[1,1,2]{2,1,0:T(1,128)} %get-tuple-element.264) | copy-start | bytes 28
  49.1 39.7 %copy-start = (bf16[128,2,128]{2,1,0:T(2,128)(2,1)S(1)}, bf16[128,2,128]{2,1,0:T(2,128)(2,1)}, u32[]{:S(2)}) copy-start(bf16[128,2,128]{2,1,0:T(2,128)(2,1)} %param.11) | copy-start | bytes 196612
  49.2 41.1 %copy-start.1 = (bf16[128,2,128]{2,1,0:T(2,128)(2,1)S(1)}, bf16[128,2,128]{2,1,0:T(2,128)(2,1)}, u32[]{:S(2)}) copy-start(bf16[128,2,128]{2,1,0:T(2,128)(2,1)} %param.12) | copy-start | bytes 196612
  67.9 33.7 %copy-start.3 = (f32[16,128]{1,0:T(8,128)S(1)}, f32[16,128]{1,0:T(8,128)}, u32[]{:S(2)}) copy-start(f32[16,128]{1,0:T(8,128)} %param.14) | copy-start | bytes 24580
Sparse Core Ops, SparseCore 0:
  11.1 43.3 all-gather.3
where the time goes:
time: 110 us
  blocking collectives  52.4 us (48%)
  other arithmetic  18.3 us (17%)
  matrix products  13.7 us (12%)
  between operations  13.6 us (12%)
  local copies, waits for them, and re-layouts  11.2 us (10%)
    all_gather x1, blocking collectives, prefix(): everything = jax.tree.map(lambda part: lax.all_gather(part, axis), shard)  20.6 us
    all_gather x1, blocking collectives, shards(): lax.all_gather(values, 'seq', axis=0, tiled=True)  16.1 us
    all_gather x1, blocking collectives, shards(): lax.all_gather(keys, 'seq', axis=0, tiled=True)  15.7 us
    select_n x8, other arithmetic, turn(): return jax.tree.map(lambda a, b: jnp.where(reached, a, b), new, before)  7.94 us
    dot_general x2, matrix products, one_block(): jnp.einsum('krqju,jukd->qkrd', weights, pv, preferred_element_type=jnp.fl...  4.6 us
    reduce_sum x2, other arithmetic, one_block(): denom = jnp.sum(expo, axis=(3, 4))  4.54 us
    dot_general x2, matrix products, one_block(): jnp.einsum('qkrd,jukd->krqju', qblk, pk, preferred_element_type=jnp.float32)  3.54 us
    unnamed x13, local copies, waits for them, and re-layouts  2.52 us
  transfers between devices with their start and end apart: 1, of which 0 were waited for; matrix products, arithmetic and copies ran while one was open for 25% of the time, Pallas kernels for 0%

commit v1 on v0

--- a/solution.py
+++ b/solution.py
@@ -6,6 +6,16 @@
 BLK = 64
 SEL = 16
 HIGH = lax.Precision.HIGHEST
+
+
+def ring_gather(x, axis, dim):
+    ways, here, lap = (lax.axis_size(axis), lax.axis_index(axis), x.shape[dim])
+    shape = [n * ways if d == dim else n for d, n in enumerate(x.shape)]
+    full = lax.dynamic_update_slice_in_dim(jnp.zeros(shape, x.dtype), x, here * lap, axis=dim)
+    for far in range(1, ways):
+        x = lax.ppermute(x, axis, [(d, (d + 1) % ways) for d in range(ways)])
+        full = lax.dynamic_update_slice_in_dim(full, x, (here - far) % ways * lap, axis=dim)
+    return full
 
 
 def prefix(shard, axis, combine, identity):
@@ -61,7 +71,7 @@
     start_pos = (lax.axis_index("seq") * n_inner + lax.axis_index("inner")) * tokens
     seg_block = block_list // (n_inner * per_piece) * per_piece + block_list % per_piece
     seg_keys, seg_values = (
-        lax.all_gather(keys, "seq", axis=0, tiled=True),
+        ring_gather(keys, "seq", 0),
         lax.all_gather(values, "seq", axis=0, tiled=True),
     )
     key_blocks = seg_keys.reshape(-1, BLK, kv_loc, width)

time: 110 us -> 106 us (0.964)
  blocking collectives: 52.4 us -> 34.2 us
  waiting for transfers between devices: 0.04 us -> 12.1 us
  local copies, waits for them, and re-layouts: 11.2 us -> 7.58 us
  starting transfers between devices: 0.01 us -> 3.17 us
  matrix products: 13.7 us -> 15.8 us
    all_gather x1 -> x0, blocking collectives: 15.7 us -> none  [shards(): lax.all_gather(keys, 'seq', axis=0, tiled=True)]
    ppermute x0 -> x3, waiting for transfers between devices: none -> 12.1 us  [ring_gather(): x = lax.ppermute(x, axis, [(d, (d + 1) % ways) for d in range(ways)])]
    ppermute x0 -> x3, starting transfers between devices: none -> 3.17 us  [ring_gather(): x = lax.ppermute(x, axis, [(d, (d + 1) % ways) for d in range(ways)])]
    all_gather x1, blocking collectives: 20.6 us -> 18.5 us  [prefix(): everything = jax.tree.map(lambda part: lax.all_gather(part, axis), shard)]
    dynamic_slice x4, local copies, waits for them, and re-layouts: 2.11 us -> 0.21 us  [shards(): lax.map(one_block, (q_blocks, picked_keys, picked_values, query_pos, key_...]
    dot_general x1, matrix products: 0.68 us -> 2.54 us  [shards(): jnp.einsum('krts,skd->tkrd', scores * weight[:, None], vf, precision=HIGH)]
    dynamic_update_slice x2, local copies, waits for them, and re-layouts: 0.7 us -> 2.21 us  [shards(): lax.map(one_block, (q_blocks, picked_keys, picked_values, query_pos, key_...]
    le x4, local copies, waits for them, and re-layouts: 1.38 us -> 0.02 us  [one_block(): valid = keep[None, :, None] & (kpos[None] <= qpos[:, None, None])]
  transfers between devices with their start and end apart: 1 -> 4, of which waited for: 0 -> 2; matrix products, arithmetic and copies ran while one was open for 25% -> 26% of each run, Pallas kernels for 0% -> 0%
where the time goes in v1:
time: 106 us; the launch traced here: 105 us
  blocking collectives  34.2 us (32%)
  other arithmetic  18.4 us (17%)
  matrix products  15.8 us (15%)
  between operations  13.6 us (13%)
  waiting for transfers between devices  12.1 us (11%)
  local copies, waits for them, and re-layouts  7.58 us (7%)
  starting transfers between devices  3.17 us (3%)
    all_gather x1, blocking collectives, prefix(): everything = jax.tree.map(lambda part: lax.all_gather(part, axis), shard)  18.5 us
    all_gather x1, blocking collectives, shards(): lax.all_gather(values, 'seq', axis=0, tiled=True)  15.7 us
    ppermute x3, waiting for transfers between devices, ring_gather(): x = lax.ppermute(x, axis, [(d, (d + 1) % ways) for d in range(ways)])  12.1 us
    select_n x8, other arithmetic, turn(): return jax.tree.map(lambda a, b: jnp.where(reached, a, b), new, before)  7.94 us
    dot_general x2, matrix products, one_block(): jnp.einsum('krqju,jukd->qkrd', weights, pv, preferred_element_type=jnp.fl...  4.55 us
    reduce_sum x2, other arithmetic, one_block(): denom = jnp.sum(expo, axis=(3, 4))  4.53 us
    dot_general x2, matrix products, one_block(): jnp.einsum('qkrd,jukd->krqju', qblk, pk, preferred_element_type=jnp.float32)  3.54 us
    ppermute x3, starting transfers between devices, ring_gather(): x = lax.ppermute(x, axis, [(d, (d + 1) % ways) for d in range(ways)])  3.17 us
  transfers between devices with their start and end apart: 4, of which 2 were waited for; matrix products, arithmetic and copies ran while one was open for 26% of the time, Pallas kernels for 0%

profile of v1, /device:TPU:0, one launch (start us, length us, event | category | flops | bytes accessed | tf_op | source)
XLA Modules:
  0.0 105.1 jit_solution(10155431566955906545)
XLA Ops:
  7.5 3.1 %collective-permute-start = (bf16[128,2,128]{2,0,1:T(8,128)(2,1)S(1)}, bf16[128,2,128]{2,0,1:T(8,128)(2,1)S(1)}, u32[]{:S(2)}, u32[]{:S(2)}) collective-permute-start(bf16[128,2,128]{2,0,1:T(8,128)(2,1)S(1)} %get-tuple-element.265), channel_id=1, source_target_pairs={{0,4},{4,8},{8,12},{12,0},{1,5},{5,9},{9,13},{13,1},{2,6},{6,10},{... | collective-permute-start | bytes 196616 | tf_op jit(solution)/shard_map/ppermute | solution.py:16
  11.6 1.0 convert_multiply_fusion
  12.7 1.8 %fusion.30 = f32[2,128,128]{2,1,0:T(8,128)} fusion(f32[128,2,128]{2,1,0:T(2,128)S(1)} %convert_multiply_fusion, bf16[128,2,128]{2,1,0:T(2,128)(2,1)} %param.12), kind=kOutput, calls=%fused_computation.44 | convolution fusion | flops 50331648 | bytes 327680 | tf_op jit(solution)/shard_map/skd,ske->kde/dot_general | solution.py:57
  16.2 15.7 %all_gather.16 = bf16[512,2,128]{2,0,1:T(8,128)(2,1)S(1)} all-gather(bf16[128,2,128]{2,0,1:T(8,128)(2,1)S(1)} %copy.123), channel_id=1, replica_groups=mesh['groups'=2,'seq'=4,'inner'=2,'head'=2] {'seq'}, dimensions={0}, use_global_device_ids=true | all-gather | bytes 327680 | tf_op jit(solution)/shard_map/all_gather | solution.py:75
  32.9 18.5 %all-gather.1 = f32[8,1,2]{2,1,0:T(1,128)S(1)} all-gather(f32[1,1,2]{2,1,0:T(1,128)S(1)} %get-tuple-element.264), channel_id=1, replica_groups=mesh['groups'=2,'seq'=4,'inner'=2,'head'=2] {'seq','inner'}, dimensions={0}, use_global_device_ids=true | all-gather | bytes 72 | tf_op jit(solution)/shard_map/all_gather | solution.py:23
  52.5 1.4 %fusion.26 = f32[2,8,128,128]{2,3,1,0:T(8,128)S(1)} fusion(f32[2,128,128]{1,2,0:T(8,128)S(1)} %exponential_select_fusion.1, bf16[128,2,8,128]{3,2,1,0:T(8,128)(2,1)} %bitcast.137, bf16[128,2,128,1]{2,1,0,3:T(2,128)(2,1)} %bitcast.143), kind=kOutput, calls=%fused_computation.38 | convolution fusion | flops 67371008 | bytes 1769472 | tf_op jit(solution)/shard_map/tkrd,skd->krts/dot_general | solution.py:52
  53.9 2.5 %convolution_bitcast_fusion.2 = f32[128,2,8,128]{0,3,2,1:T(8,128)} fusion(f32[2,8,128,128]{2,3,1,0:T(8,128)S(1)} %fusion.26, bf16[128,2,128,1]{2,1,0,3:T(2,128)(2,1)} %bitcast.144), kind=kOutput, calls=%fused_computation.37 | convolution fusion | flops 402653184 | bytes 2162688 | tf_op jit(solution)/shard_map/krts,skd->tkrd/dot_general | solution.py:55
  56.5 6.0 %collective-permute-done.1 = bf16[128,2,128]{2,0,1:T(8,128)(2,1)S(1)} collective-permute-done((bf16[128,2,128]{2,0,1:T(8,128)(2,1)S(1)}, bf16[128,2,128]{2,0,1:T(8,128)(2,1)S(1)}, u32[]{:S(2)}, u32[]{:S(2)}) %collective-permute-start.1) | collective-permute-done | bytes 65568 | tf_op jit(solution)/shard_map/ppermute | solution.py:16
  62.6 6.0 %collective-permute-done.2 = bf16[128,2,128]{2,0,1:T(8,128)(2,1)S(1)} collective-permute-done((bf16[128,2,128]{2,0,1:T(8,128)(2,1)S(1)}, bf16[128,2,128]{2,0,1:T(8,128)(2,1)S(1)}, u32[]{:S(2)}, u32[]{:S(2)}) %collective-permute-start.2) | collective-permute-done | bytes 65568 | tf_op jit(solution)/shard_map/ppermute | solution.py:16
  69.4 15.7 %while.24 = (s32[]{:T(128)}, f32[2,64,2,8,128]{4,3,2,1,0:T(8,128)}, bf16[2,16,64,2,128]{4,2,3,1,0:T(8,128)(2,1)S(1)}, pred[2,16]{1,0:T(4,128)(4,1)S(1)}, s32[2,1...) while((s32[]{:T(128)}, f32[2,64,2,8,128]{4,3,2,1,0:T(8,128)}, ...), condition=%wide.region_8.9_spmd, body=%wide.region_5.8_spmd.sunk | while | flops 550762496 | bytes 18384288 | solution.py:102
  69.9 1.8 %fusion.50 = (f32[2,8,64]{2,1,0:T(8,128)S(1)}, f32[2,16,64,64,8]{3,2,4,1,0:T(8,128)S(1)}) fusion(pred[64,16,64]{0,2,1:T(8,128)(4,1)S(1)} %compare_and_fusion.2, bf16[1,64,2,8,128]{4,3,2,1,0:T(8,128)(2,1)S(1)} %constant_dynamic-slice_fusion.7, bf16[1,16,64,2,128]{4,2,3,1,0:T(8,128)(2,1)S(1)} %get-tuple-element.350), kind=kOutput, calls=%fused_computation.4.clone.1 | convolution fusion | flops 271580160 | bytes 5050368 | tf_op jit(solution)/shard_map/while/body/eval_jaxpr/qkrd,jukd->krqju/dot_general | solution.py:91
  71.6 2.3 %fusion.51 = f32[2,8,64]{2,1,0:T(8,128)S(1)} fusion(f32[2,16,64,64,8]{3,2,4,1,0:T(8,128)S(1)} %get-tuple-element.351, f32[2,8,64]{2,1,0:T(8,128)S(1)} %get-tuple-element.352, pred[64,16,64]{0,2,1:T(8,128)(4,1)S(1)} %compare_and_fusion.2), kind=kLoop, calls=%fused_computation.5.clone.1 | loop fusion | flops 5241856 | bytes 4268032 | tf_op jit(solution)/shard_map/while/body/eval_jaxpr/reduce_sum | solution.py:97
  73.9 2.3 %fusion.52 = f32[1,64,2,8,128]{4,1,3,2,0:T(8,128)S(1)} fusion(f32[2,16,64,64,8]{3,2,4,1,0:T(8,128)S(1)} %get-tuple-element.351, f32[2,8,64]{2,1,0:T(8,128)S(1)} %get-tuple-element.352, pred[64,16,64]{0,2,1:T(8,128)(4,1)S(1)} %compare_and_fusion.2, bf16[1,16,64,2,128]{4,2,3,1,0:T(8,128)(2,1)S(1)} %get-tuple-element.353, f32[64,2,8]{0,2,1:T(8,128)S(1)} %bitcast.147), kind=kOutput, calls=%fused_computation.11.clone.1 | convolution fusion | flops 273809408 | bytes 5316608 | tf_op jit(solution)/shard_map/while/body/eval_jaxpr/krqju,jukd->qkrd/dot_general | solution.py:99
  76.2 1.1 %copy_dynamic-update-slice_fusion.2 = f32[2,64,2,8,128]{4,3,2,1,0:T(8,128)} fusion(f32[2,64,2,8,128]{4,3,2,1,0:T(8,128)} %get-tuple-element.369, s32[]{:T(128)} %get-tuple-element.368, f32[1,64,2,8,128]{4,1,3,2,0:T(8,128)S(1)} %fusion.52), kind=kLoop, calls=%fused_computation.13.clone.1 | loop fusion | bytes 1049088 | tf_op jit(solution)/shard_map/while/body/jit(dynamic_update_index_in_dim)/dynamic_update_slice | solution.py:102
  77.7 1.8 %fusion.50 = (f32[2,8,64]{2,1,0:T(8,128)S(1)}, f32[2,16,64,64,8]{3,2,4,1,0:T(8,128)S(1)}) fusion(pred[64,16,64]{0,2,1:T(8,128)(4,1)S(1)} %compare_and_fusion.2, bf16[1,64,2,8,128]{4,3,2,1,0:T(8,128)(2,1)S(1)} %constant_dynamic-slice_fusion.7, bf16[1,16,64,2,128]{4,2,3,1,0:T(8,128)(2,1)S(1)} %get-tuple-element.350), kind=kOutput, calls=%fused_computation.4.clone.1 | convolution fusion | flops 271580160 | bytes 5050368 | tf_op jit(solution)/shard_map/while/body/eval_jaxpr/qkrd,jukd->krqju/dot_general | solution.py:91
  79.4 2.3 %fusion.51 = f32[2,8,64]{2,1,0:T(8,128)S(1)} fusion(f32[2,16,64,64,8]{3,2,4,1,0:T(8,128)S(1)} %get-tuple-element.351, f32[2,8,64]{2,1,0:T(8,128)S(1)} %get-tuple-element.352, pred[64,16,64]{0,2,1:T(8,128)(4,1)S(1)} %compare_and_fusion.2), kind=kLoop, calls=%fused_computation.5.clone.1 | loop fusion | flops 5241856 | bytes 4268032 | tf_op jit(solution)/shard_map/while/body/eval_jaxpr/reduce_sum | solution.py:97
  81.7 2.3 %fusion.52 = f32[1,64,2,8,128]{4,1,3,2,0:T(8,128)S(1)} fusion(f32[2,16,64,64,8]{3,2,4,1,0:T(8,128)S(1)} %get-tuple-element.351, f32[2,8,64]{2,1,0:T(8,128)S(1)} %get-tuple-element.352, pred[64,16,64]{0,2,1:T(8,128)(4,1)S(1)} %compare_and_fusion.2, bf16[1,16,64,2,128]{4,2,3,1,0:T(8,128)(2,1)S(1)} %get-tuple-element.353, f32[64,2,8]{0,2,1:T(8,128)S(1)} %bitcast.147), kind=kOutput, calls=%fused_computation.11.clone.1 | convolution fusion | flops 273809408 | bytes 5316608 | tf_op jit(solution)/shard_map/while/body/eval_jaxpr/krqju,jukd->qkrd/dot_general | solution.py:99
  84.0 1.1 %copy_dynamic-update-slice_fusion.2 = f32[2,64,2,8,128]{4,3,2,1,0:T(8,128)} fusion(f32[2,64,2,8,128]{4,3,2,1,0:T(8,128)} %get-tuple-element.369, s32[]{:T(128)} %get-tuple-element.368, f32[1,64,2,8,128]{4,1,3,2,0:T(8,128)S(1)} %fusion.52), kind=kLoop, calls=%fused_computation.13.clone.1 | loop fusion | bytes 1049088 | tf_op jit(solution)/shard_map/while/body/jit(dynamic_update_index_in_dim)/dynamic_update_slice | solution.py:102
  85.1 8.2 %while.25 = (s32[]{:T(128)}, f32[2,128,128]{2,1,0:T(8,128)S(1)}, s32[]{:T(128)}, f32[8,2]{1,0:T(8,128)S(1)}, f32[8,2,128,128]{3,2,1,0:T(8,128)}, /*index=5*/s32[]{:T(128)}, s32[]{:T(128)}) while((s32[]{:T(128)}, f32[2,128,128]{2,1,0:T(8,128)S(1)}, s32[]{:T(128)}, f32[8,2]{1,0:T(8,128)S(1)}, f32[8,2,128,128]{3,2,1,0:T(8,128)}, ...), condition=%wide.region_2.3_spmd.clone, body=%wide.region_1.2_spmd.clone.sunk | while | flops 131076 | bytes 393345 | solution.py:35
  85.1 1.0 fusion.53
  86.2 1.0 fusion.53
  87.2 1.0 fusion.53
  93.4 1.9 %multiply_reduce_fusion = (f32[128,2,8]{0,2,1:T(8,128)S(1)}, f32[128,2,8,128]{0,3,2,1:T(8,128)S(1)}) fusion(f32[128,2,8,128]{0,3,2,1:T(8,128)} %convolution_bitcast_fusion.2, bf16[128,2,8,128]{3,2,1,0:T(8,128)(2,1)S(1)} %bitcast.139, f32[2,128,128]{2,1,0:T(8,128)S(1)} %get-tuple-element.141, f32[128,2]{0,1:T(2,128)S(1)} %copy.120), kind=kOutput, calls=%fused_computation.40 | convolution fusion | flops 403699712 | bytes 2761728 | tf_op jit(solution)/shard_map/tkrd,kde->tkre/dot_general | solution.py:62
  95.9 2.4 %add_convert_fusion = bf16[128,16,128]{2,1,0:T(8,128)(2,1)} fusion(f32[128,16,128]{2,1,0:T(8,128)} %bitcast.38, f32[128,16,128]{2,1,0:T(8,128)S(1)} %copy.128, f32[16,128]{1,0:T(8,128)S(1)} %copy-done.1, f32[128,16]{1,0:T(8,128)S(1)} %copy.127), kind=kLoop, calls=%fused_computation.39 | loop fusion | flops 1048576 | bytes 2637824 | tf_op jit(solution)/shard_map/convert_element_type | solution.py:104
  (66 shorter events, 12.9 us)
Async XLA Ops:
  6.5 62.9 %copy-start = (bf16[128,16,128]{2,1,0:T(8,128)(2,1)S(1)}, bf16[128,16,128]{2,1,0:T(8,128)(2,1)}, u32[]{:S(2)}) copy-start(bf16[128,16,128]{2,1,0:T(8,128)(2,1)} %param.10) | copy-start | bytes 1572868
  6.5 78.6 %all-gather.4.cloned.1.call-start = ((), (), s32[]{:S(2)}) async-start(), calls=%async_computation | async-start | bytes 1179648 | tf_op jit(solution)/shard_map/all_gather | solution.py:23
  7.5 48.9 %collective-permute-start = (bf16[128,2,128]{2,0,1:T(8,128)(2,1)S(1)}, bf16[128,2,128]{2,0,1:T(8,128)(2,1)S(1)}, u32[]{:S(2)}, u32[]{:S(2)}) collective-permute-start(bf16[128,2,128]{2,0,1:T(8,128)(2,1)S(1)} %get-tuple-element.265), channel_id=1, source_target_pairs={{0,4},{4,8},{8,12},{12,0},{1,5},{5,9},{9,13},{13,1},{2,6},{6,10},{... | collective-permute-start | bytes 196616 | tf_op jit(solution)/shard_map/ppermute | solution.py:16
  56.4 6.1 %collective-permute-start.1 = (bf16[128,2,128]{2,0,1:T(8,128)(2,1)S(1)}, bf16[128,2,128]{2,0,1:T(8,128)(2,1)S(1)}, u32[]{:S(2)}, u32[]{:S(2)}) collective-permute-start(bf16[128,2,128]{2,0,1:T(8,128)(2,1)S(1)} %collective-permute-done), channel_id=1, source_target_pairs={{0,4},{4,8},{8,12},{12,0},{1,5},{5,9},{9,13},{13,1},{2,6},{6,10},{... | collective-permute-start | bytes 196616 | tf_op jit(solution)/shard_map/ppermute | solution.py:16
  62.6 6.1 %collective-permute-start.2 = (bf16[128,2,128]{2,0,1:T(8,128)(2,1)S(1)}, bf16[128,2,128]{2,0,1:T(8,128)(2,1)S(1)}, u32[]{:S(2)}, u32[]{:S(2)}) collective-permute-start(bf16[128,2,128]{2,0,1:T(8,128)(2,1)S(1)} %collective-permute-done.1), channel_id=1, source_target_pairs={{0,4},{4,8},{8,12},{12,0},{1,5},{5,9},{9,13},{13,1},{2,6},{6,10},{... | collective-permute-start | bytes 196616 | tf_op jit(solution)/shard_map/ppermute | solution.py:16
  69.4 26.5 %copy-start.1 = (f32[16,128]{1,0:T(8,128)S(1)}, f32[16,128]{1,0:T(8,128)}, u32[]{:S(2)}) copy-start(f32[16,128]{1,0:T(8,128)} %param.14) | copy-start | bytes 24580
Sparse Core Ops, SparseCore 0:
  14.6 41.6 all-gather.3
